TPU v7x, 32 devices: a whole 2x2x4 slice. The times are simulated.
32 devices in a mesh: row: 8 (over z, core), col: 4 (over y, x).
Axes of the slice: x: 2, y: 2, z: 4, core: 2. Of those that a mesh axis runs over, the one named last changes fastest.
Arguments:
- coeffs: bfloat16 [256, 64, 128], P(('row', 'col')), may hold values from -6 to 6
- blocks: bfloat16 [16384, 64, 64], P(('row', 'col')), may hold values from -0.046875 to 0.046875
- blk_rows: int32 [16384], P(('row', 'col')), may hold values from 0 to 255, as said below
- blk_cols: int32 [16384], P(('row', 'col')), may hold values from 0 to 255, as said below
- blk_count: int32 [32], P(('row', 'col')), may hold values from 0 to 512, as said below
Outputs:
- product: float32 [256, 64, 128], P(('row', 'col'))
Inputs may be any that keep to these rules, and one draw needn't show every extreme that they name: `blk_rows`: element e belongs to device e // 8 in row+col order. In the first blk_count slots of a device, I <= J, I belongs to a device of the same row index, and J to a device of the same column index whose row index exceeds that of I's device by 0 to 3; the difference 3 occurs in every draw. Later slots hold elements of the device's own row and column groups and are unused; pairs may repeat. `blk_cols`: see blk_rows. `blk_count`: counts differ widely between devices; some device uses all 512 slots in every draw.
All inputs are finite; a program needn't handle non-finite values.
Results may differ from a plain program's by a relative error of at most 0.0003.
Values may be sent and summed in bfloat16 or wider, within the bound.
No kernel may reach another device: no remote copies, remote signals or barrier semaphores. Data moves between devices by JAX's collectives and lax.ppermute only.
A program may use at most 128 MiB of HBM per device.

v0:
```python
import jax
import jax.numpy as jnp
from jax import lax
from jax.sharding import PartitionSpec as P

REACH = 3


def from_behind(block, axis, distance):
    devices = range(lax.axis_size(axis))
    route = [(i - distance, i) for i in devices if i - distance in devices]
    return lax.ppermute(block, axis, route)


def body(coeffs, blocks, blk_rows, blk_cols, blk_count):
    high_precision = lax.Precision.HIGHEST
    elem_dev, width, sides = coeffs.shape
    slot_total = blocks.shape[0]
    my_row = lax.axis_index("row")
    segment = elem_dev * lax.axis_size("col")
    window = (REACH + 1) * elem_dev
    row_group = lax.all_gather(coeffs, "col", axis=0, tiled=True)
    gathered = coeffs
    spread = 1
    for level in range(REACH.bit_length()):
        arrived = from_behind(gathered, "row", -spread)
        gathered = jnp.concatenate([gathered, arrived], axis=0)
        spread = spread * 2
    active = jnp.arange(slot_total, dtype=jnp.int32) < blk_count[0]
    mirror = active & (blk_rows != blk_cols)
    row_local = jnp.clip(blk_rows - my_row * segment, 0, segment - 1)
    col_local = (blk_cols // segment - my_row) * elem_dev + blk_cols % elem_dev
    col_local = jnp.clip(col_local, 0, window - 1)
    column_entries = gathered[col_local]
    row_contributions = jnp.einsum(
        "gjc,gcx->gjx", blocks, column_entries, preferred_element_type=jnp.float32
    )
    row_contributions = row_contributions.reshape(slot_total, width * sides)
    row_select = (
        (row_local[None, :] == jnp.arange(segment, dtype=jnp.int32)[:, None]) & active[None, :]
    ).astype(jnp.float32)
    row_entries = row_group[row_local]
    column_contributions = jnp.einsum(
        "ihv,ihe->ive", blocks, row_entries, preferred_element_type=jnp.float32
    )
    column_contributions = column_contributions.reshape(slot_total, width * sides)
    col_select = (
        (col_local[None, :] == jnp.arange(window, dtype=jnp.int32)[:, None]) & mirror[None, :]
    ).astype(jnp.float32)
    col_part = jnp.dot(
        col_select,
        column_contributions,
        precision=high_precision,
        preferred_element_type=jnp.float32,
    )
    row_part = jnp.dot(
        row_select, row_contributions, precision=high_precision, preferred_element_type=jnp.float32
    )
    row_sums = lax.psum_scatter(row_part, "col", scatter_dimension=0, tiled=True)
    col_sums = col_part[:elem_dev]
    for offset in range(1, REACH + 1):
        piece = col_part[offset * elem_dev : (offset + 1) * elem_dev]
        col_sums = col_sums + from_behind(piece, "row", offset)
    return (row_sums + col_sums).reshape(elem_dev, width, sides)


def solution(mesh):
    placed = (
        P(("row", "col"), None, None),
        P(("row", "col"), None, None),
        P(("row", "col")),
        P(("row", "col")),
        P(("row", "col")),
    )
    return jax.shard_map(
        body, mesh=mesh, in_specs=placed, out_specs=P(("row", "col"), None, None), check_vma=False
    )
```

profile of v0, /device:TPU:0, one launch (start us, length us, event | category | flops | bytes accessed | tf_op | source)
XLA Modules:
  0.0 199.8 jit_solution(3817646635028299067)
XLA Ops:
  6.5 0.0 copy-start.2
  6.5 0.0 all-reduce.3.cloned.1.call-start
  6.5 1.4 collective-permute-start
  8.0 13.1 %all_gather.3 = bf16[32,64,128]{2,1,0:T(8,128)(2,1)S(1)} all-gather(bf16[8,64,128]{2,1,0:T(8,128)(2,1)} %param.5), channel_id=1, replica_groups=mesh['row'=8,'col'=4] {'col'}, dimensions={0}, use_global_device_ids=true | all-gather | bytes 655360 | tf_op jit(solution)/shard_map/all_gather | solution.py:22
  21.1 0.7 compare_select_fusion
  21.8 15.7 %copy.10 = bf16[512,64,64]{1,2,0:T(8,128)(2,1)} copy(bf16[512,64,64]{0,2,1:T(8,128)(2,1)} %param.6) | data formatting | bytes 8388608 | tf_op args[1]
  37.4 0.0 copy-done.2
  38.1 13.4 %gather_fusion.1 = bf16[512,64,128]{2,1,0:T(8,128)(2,1)} fusion(bf16[32,64,128]{2,1,0:T(8,128)(2,1)S(1)} %all_gather.3, s32[1024]{0:T(1024)S(1)} %pad_clamp_fusion), kind=kCustom, calls=%fused_computation.1 | custom fusion | bytes 16779264 | tf_op jit(solution)/shard_map/gather | solution.py:42
  51.5 13.9 %fusion.28 = f32[512,128,64]{1,2,0:T(8,128)} fusion(bf16[512,64,64]{1,2,0:T(8,128)(2,1)} %copy.10, bf16[512,64,128]{2,1,0:T(8,128)(2,1)} %gather_fusion.1), kind=kOutput, calls=%fused_computation.46 | convolution fusion | flops 536870912 | bytes 29360128 | tf_op jit(solution)/shard_map/ihv,ihe->ive/dot_general | solution.py:43
  65.4 0.0 copy-done.1
  65.4 0.0 collective-permute-done
  65.4 0.0 copy-done
  65.5 1.5 collective-permute-start.1
  66.9 20.3 %fusion = f32[32,8192]{1,0:T(8,128)S(1)} fusion(f32[64,8,64,128]{3,2,1,0:T(8,128)} %bitcast.20, s32[512]{0:T(512)S(1)} %get-tuple-element.6, pred[512]{0:T(512)(128)(4,1)S(1)} %compare_and_fusion), kind=kOutput, calls=%fused_computation.2 | convolution fusion | flops 1610645504 | bytes 17828352 | tf_op jit(solution)/shard_map/dot_general | solution.py:50
  87.3 0.0 collective-permute-done.1
  87.3 0.1 pad_maximum_fusion
  87.4 13.6 %gather_fusion = bf16[512,64,128]{2,1,0:T(8,128)(2,1)} fusion(bf16[32,64,128]{2,1,0:T(8,128)(2,1)S(1)} %pad_maximum_fusion, s32[1024]{0:T(1024)S(1)} %pad_clamp_fusion.1), kind=kCustom, calls=%fused_computation | custom fusion | bytes 16779264 | tf_op jit(solution)/shard_map/gather | solution.py:34
  101.0 14.4 %fusion.27 = f32[512,128,64]{1,2,0:T(8,128)} fusion(bf16[512,64,64]{1,2,0:T(8,128)(2,1)} %copy.10, bf16[512,64,128]{2,1,0:T(8,128)(2,1)} %gather_fusion), kind=kOutput, calls=%fused_computation.45 | convolution fusion | flops 536870912 | bytes 29360128 | tf_op jit(solution)/shard_map/gjc,gcx->gjx/dot_general | solution.py:35
  115.4 21.2 %fusion.3 = f32[32,8192]{1,0:T(8,128)} fusion(f32[64,8,64,128]{3,2,1,0:T(8,128)} %bitcast.21, s32[512]{0:T(512)S(1)} %get-tuple-element.8, pred[512]{0:T(512)(128)(4,1)S(1)} %iota_compare_fusion.2), kind=kOutput, calls=%fused_computation.5 | convolution fusion | flops 1610645504 | bytes 17828352 | tf_op jit(solution)/shard_map/dot_general | solution.py:56
  136.6 0.0 all-reduce.3.cloned.1.call-update
  136.6 0.1 fusion.26
  136.7 1.6 collective-permute-start.2
  138.3 5.0 %collective-permute-start.3 = (f32[8,8192]{1,0:T(8,128)S(1)}, f32[8,8192]{1,0:T(8,128)S(1)}, u32[]{:S(2)}, u32[]{:S(2)}) collective-permute-start(f32[8,8192]{1,0:T(8,128)S(1)} %get-tuple-element.11), channel_id=1, source_target_pairs={{0,8},{4,12},{8,16},{12,20},{16,24},{20,28},{1,9},{5,13},{9,17},{1... | collective-permute-start | bytes 786440 | tf_op jit(solution)/shard_map/ppermute | solution.py:12
  143.3 4.9 %collective-permute-start.4 = (f32[8,8192]{1,0:T(8,128)S(1)}, f32[8,8192]{1,0:T(8,128)S(1)}, u32[]{:S(2)}, u32[]{:S(2)}) collective-permute-start(f32[8,8192]{1,0:T(8,128)S(1)} %get-tuple-element.10), channel_id=1, source_target_pairs={{0,12},{4,16},{8,20},{12,24},{16,28},{1,13},{5,17},{9,21},{13,25},... | collective-permute-start | bytes 786440 | tf_op jit(solution)/shard_map/ppermute | solution.py:12
  148.2 0.0 copy-done.3
  148.2 0.6 dynamic-slice
  149.5 0.0 collective-permute-done.2
  149.5 0.0 collective-permute-done.3
  149.5 5.6 %collective-permute-done.4 = f32[8,8192]{1,0:T(8,128)S(1)} collective-permute-done((f32[8,8192]{1,0:T(8,128)S(1)}, f32[8,8192]{1,0:T(8,128)S(1)}, u32[]{:S(2)}, u32[]{:S(2)}) %collective-permute-start.4) | collective-permute-done | bytes 262176 | tf_op jit(solution)/shard_map/ppermute | solution.py:12
  155.1 36.1 %all-reduce.3.cloned.1.call-done = f32[32,8192]{1,0:T(8,128)} async-done(((f32[32,8192]{1,0:T(8,128)}), f32[32,8192]{1,0:T(8,128)}) %all-reduce.3.cloned.1.call-update) | async-done | bytes 1048592
  191.1 1.0 fusion.9
  192.2 0.8 copy.11
  (9 shorter events, 0.1 us)
Async XLA Ops:
  6.5 30.9 %copy-start.2 = (s32[512]{0:T(512)S(1)}, s32[512]{0:T(512)}, u32[]{:S(2)}) copy-start(s32[512]{0:T(512)} %param.8) | copy-start | bytes 6148
  6.5 184.6 %all-reduce.3.cloned.1.call-start = ((), (), s32[]{:S(2)}) async-start(), calls=%async_computation | async-start | bytes 2097152
  6.5 58.9 %collective-permute-start = (bf16[8,64,128]{2,1,0:T(8,128)(2,1)}, bf16[8,64,128]{2,1,0:T(8,128)(2,1)S(1)}, u32[]{:S(2)}, u32[]{:S(2)}) collective-permute-start(bf16[8,64,128]{2,1,0:T(8,128)(2,1)} %param.5), channel_id=1, source_target_pairs={{4,0},{8,4},{12,8},{16,12},{20,16},{24,20},{28,24},{5,1},{9,5},{13... | collective-permute-start | bytes 393224 | tf_op jit(solution)/shard_map/ppermute | solution.py:12
  51.5 13.9 %copy-start.1 = (s32[512]{0:T(512)S(1)}, s32[512]{0:T(512)}, u32[]{:S(2)}) copy-start(s32[512]{0:T(512)} %param.7) | copy-start | bytes 6148
  51.5 13.9 %copy-start = (bf16[8,64,128]{2,1,0:T(8,128)(2,1)S(1)}, bf16[8,64,128]{2,1,0:T(8,128)(2,1)}, u32[]{:S(2)}) copy-start(bf16[8,64,128]{2,1,0:T(8,128)(2,1)} %param.5) | copy-start | bytes 393220
  65.5 21.9 %collective-permute-start.1 = (bf16[16,64,128]{2,1,0:T(8,128)(2,1)S(1)}, bf16[16,64,128]{2,1,0:T(8,128)(2,1)S(1)}, u32[]{:S(2)}, u32[]{:S(2)}) collective-permute-start(bf16[16,64,128]{2,1,0:T(8,128)(2,1)S(1)} %pad_maximum_fusion.1), channel_id=1, source_target_pairs={{8,0},{12,4},{16,8},{20,12},{24,16},{28,20},{9,1},{13,5},{17,9},{2... | collective-permute-start | bytes 786440 | tf_op jit(solution)/shard_map/ppermute | solution.py:12
  115.4 32.8 %copy-start.3 = (u32[32]{0:T(128)S(1)}, u32[32]{0:T(128)}, u32[]{:S(2)}) copy-start(u32[32]{0:T(128)} %constant.46) | copy-start | bytes 388
  136.7 12.8 %collective-permute-start.2 = (f32[8,8192]{1,0:T(8,128)S(1)}, f32[8,8192]{1,0:T(8,128)S(1)}, u32[]{:S(2)}, u32[]{:S(2)}) collective-permute-start(f32[8,8192]{1,0:T(8,128)S(1)} %get-tuple-element.9), channel_id=1, source_target_pairs={{0,4},{4,8},{8,12},{12,16},{16,20},{20,24},{24,28},{1,5},{5,9},{9,... | collective-permute-start | bytes 786440 | tf_op jit(solution)/shard_map/ppermute | solution.py:12
  138.3 11.2 %collective-permute-start.3 = (f32[8,8192]{1,0:T(8,128)S(1)}, f32[8,8192]{1,0:T(8,128)S(1)}, u32[]{:S(2)}, u32[]{:S(2)}) collective-permute-start(f32[8,8192]{1,0:T(8,128)S(1)} %get-tuple-element.11), channel_id=1, source_target_pairs={{0,8},{4,12},{8,16},{12,20},{16,24},{20,28},{1,9},{5,13},{9,17},{1... | collective-permute-start | bytes 786440 | tf_op jit(solution)/shard_map/ppermute | solution.py:12
  143.3 11.8 %collective-permute-start.4 = (f32[8,8192]{1,0:T(8,128)S(1)}, f32[8,8192]{1,0:T(8,128)S(1)}, u32[]{:S(2)}, u32[]{:S(2)}) collective-permute-start(f32[8,8192]{1,0:T(8,128)S(1)} %get-tuple-element.10), channel_id=1, source_target_pairs={{0,12},{4,16},{8,20},{12,24},{16,28},{1,13},{5,17},{9,21},{13,25},... | collective-permute-start | bytes 786440 | tf_op jit(solution)/shard_map/ppermute | solution.py:12
Sparse Core Ops, SparseCore 0:
  136.8 54.3 all-reduce.2
where the time goes:
time: 200 us
  matrix products  69.8 us (35%)
  local copies, waits for them, and re-layouts  44.1 us (22%)
  waiting for transfers between devices  41.7 us (21%)
  between operations  14.8 us (7%)
  starting transfers between devices  14.4 us (7%)
  blocking collectives  13.1 us (7%)
    unnamed x2, waiting for transfers between devices  36.1 us
    dot_general x1, matrix products, body(): jnp.dot(row_select, row_contributions, precision=high_precision, preferre...  21.2 us
    dot_general x1, matrix products, body(): jnp.dot(col_select, column_contributions, precision=high_precision, prefe...  20.3 us
    unnamed x10, local copies, waits for them, and re-layouts  16.3 us
    dot_general x1, matrix products, body(): jnp.einsum('gjc,gcx->gjx', blocks, column_entries, preferred_element_type...  14.4 us
    ppermute x5, starting transfers between devices, from_behind(): return lax.ppermute(block, axis, route)  14.4 us
    dot_general x1, matrix products, body(): jnp.einsum('ihv,ihe->ive', blocks, row_entries, preferred_element_type=jn...  13.9 us
    gather x1, local copies, waits for them, and re-layouts, body(): column_entries = gathered[col_local]  13.6 us
  transfers between devices with their start and end apart: 6, of which 2 were waited for; matrix products, arithmetic and copies ran while one was open for 32% of the time, Pallas kernels for 0%

commit v1 on v0

--- a/solution.py
+++ b/solution.py
@@ -19,7 +19,16 @@
     my_row = lax.axis_index("row")
     segment = elem_dev * lax.axis_size("col")
     window = (REACH + 1) * elem_dev
-    row_group = lax.all_gather(coeffs, "col", axis=0, tiled=True)
+    value = coeffs
+    ways, here, step = (lax.axis_size("col"), lax.axis_index("col"), value.shape[0])
+    shape = [n * ways if d == 0 else n for d, n in enumerate(value.shape)]
+    full = lax.dynamic_update_slice_in_dim(
+        jnp.zeros(shape, value.dtype), value, here * step, axis=0
+    )
+    for far in range(1, ways):
+        value = lax.ppermute(value, "col", [(d, (d + 1) % ways) for d in range(ways)])
+        full = lax.dynamic_update_slice_in_dim(full, value, (here - far) % ways * step, axis=0)
+    row_group = full
     gathered = coeffs
     spread = 1
     for level in range(REACH.bit_length()):

time: 200 us -> 179 us (0.90)
  waiting for transfers between devices: 41.7 us -> 25.8 us
  blocking collectives: 13.1 us -> 0 us
  starting transfers between devices: 14.4 us -> 19.5 us
    unnamed x2, waiting for transfers between devices: 36.1 us -> 13.7 us
    all_gather x1 -> x0, blocking collectives: 13.1 us -> none  [body(): row_group = lax.all_gather(coeffs, 'col', axis=0, tiled=True)]
    ppermute x0 -> x3, starting transfers between devices: none -> 6.23 us  [body(): lax.ppermute(value, 'col', [(d, (d + 1) % ways) for d in range(ways)])]
    ppermute x0 -> x3, waiting for transfers between devices: none -> 5.61 us  [body(): lax.ppermute(value, 'col', [(d, (d + 1) % ways) for d in range(ways)])]
    unnamed x10 -> x6, local copies, waits for them, and re-layouts: 16.3 us -> 16.3 us
  transfers between devices with their start and end apart: 6 -> 9, of which waited for: 2 -> 4; matrix products, arithmetic and copies ran while one was open for 32% -> 38% of each run, Pallas kernels for 0% -> 0%
where the time goes in v1:
time: 179 us
  matrix products  70 us (39%)
  local copies, waits for them, and re-layouts  45.2 us (25%)
  waiting for transfers between devices  25.8 us (14%)
  starting transfers between devices  19.5 us (11%)
  between operations  14.9 us (8%)
  other arithmetic  3.2 us (2%)
    dot_general x1, matrix products, body(): jnp.dot(row_select, row_contributions, precision=high_precision, preferre...  21.2 us
    dot_general x1, matrix products, body(): jnp.dot(col_select, column_contributions, precision=high_precision, prefe...  20.6 us
    unnamed x6, local copies, waits for them, and re-layouts  16.3 us
    dot_general x1, matrix products, body(): jnp.einsum('gjc,gcx->gjx', blocks, column_entries, preferred_element_type...  14.4 us
    dot_general x1, matrix products, body(): jnp.einsum('ihv,ihe->ive', blocks, row_entries, preferred_element_type=jn...  13.8 us
    unnamed x2, waiting for transfers between devices  13.7 us
    gather x1, local copies, waits for them, and re-layouts, body(): column_entries = gathered[col_local]  13.5 us
    gather x1, local copies, waits for them, and re-layouts, body(): row_entries = row_group[row_local]  13.5 us
  transfers between devices with their start and end apart: 9, of which 4 were waited for; matrix products, arithmetic and copies ran while one was open for 38% of the time, Pallas kernels for 0%

profile of v1, /device:TPU:0, one launch (start us, length us, event | category | flops | bytes accessed | tf_op | source)
XLA Modules:
  0.0 178.5 jit_solution(15841369825017157357)
XLA Ops:
  6.5 3.0 %collective-permute-start.2 = (bf16[8,64,128]{2,1,0:T(8,128)(2,1)}, bf16[8,64,128]{2,1,0:T(8,128)(2,1)S(1)}, u32[]{:S(2)}, u32[]{:S(2)}) collective-permute-start(bf16[8,64,128]{2,1,0:T(8,128)(2,1)} %param.5), channel_id=1, source_target_pairs={{0,1},{1,2},{2,3},{3,0},{4,5},{5,6},{6,7},{7,4},{8,9},{9,10},{10,1... | collective-permute-start | bytes 393224 | tf_op jit(solution)/shard_map/ppermute | solution.py:29
  9.5 1.3 collective-permute-start
  10.8 0.7 compare_select_fusion.1
  12.2 0.7 compare_select_fusion
  12.8 0.7 compare_and_fusion
  13.5 0.1 broadcast_in_dim.7
  13.7 0.9 constant_dynamic-update-slice_fusion.3
  14.6 1.5 collective-permute-start.3
  16.2 15.7 %copy.10 = bf16[512,64,64]{1,2,0:T(8,128)(2,1)} copy(bf16[512,64,64]{0,2,1:T(8,128)(2,1)} %param.6) | data formatting | bytes 8388608 | tf_op args[1]
  31.9 1.3 collective-permute-start.1
  33.2 0.0 collective-permute-done.3
  33.2 1.7 collective-permute-start.4
  35.0 5.6 %collective-permute-done.4 = bf16[8,64,128]{2,1,0:T(8,128)(2,1)S(1)} collective-permute-done((bf16[8,64,128]{2,1,0:T(8,128)(2,1)S(1)}, bf16[8,64,128]{2,1,0:T(8,128)(2,1)S(1)}, u32[]{:S(2)}, u32[]{:S(2)}) %collective-permute-start.4) | collective-permute-done | bytes 131104 | tf_op jit(solution)/shard_map/ppermute | solution.py:29
  40.6 13.5 %gather_fusion.1 = bf16[512,64,128]{2,1,0:T(8,128)(2,1)} fusion(bf16[32,64,128]{2,1,0:T(8,128)(2,1)S(1)} %constant_dynamic-update-slice_fusion, s32[1024]{0:T(1024)S(1)} %pad_clamp_fusion), kind=kCustom, calls=%fused_computation.1 | custom fusion | bytes 16779264 | tf_op jit(solution)/shard_map/gather | solution.py:51
  54.1 13.8 %fusion.28 = f32[512,128,64]{1,2,0:T(8,128)} fusion(bf16[512,64,64]{1,2,0:T(8,128)(2,1)} %copy.10, bf16[512,64,128]{2,1,0:T(8,128)(2,1)} %gather_fusion.1), kind=kOutput, calls=%fused_computation.50 | convolution fusion | flops 536870912 | bytes 29360128 | tf_op jit(solution)/shard_map/ihv,ihe->ive/dot_general | solution.py:52
  67.9 0.1 pad_maximum_fusion
  67.9 13.5 %gather_fusion = bf16[512,64,128]{2,1,0:T(8,128)(2,1)} fusion(bf16[32,64,128]{2,1,0:T(8,128)(2,1)S(1)} %pad_maximum_fusion, s32[1024]{0:T(1024)S(1)} %pad_clamp_fusion.1), kind=kCustom, calls=%fused_computation | custom fusion | bytes 16779264 | tf_op jit(solution)/shard_map/gather | solution.py:43
  81.5 14.4 %fusion.27 = f32[512,128,64]{1,2,0:T(8,128)} fusion(bf16[512,64,64]{1,2,0:T(8,128)(2,1)} %copy.10, bf16[512,64,128]{2,1,0:T(8,128)(2,1)} %gather_fusion), kind=kOutput, calls=%fused_computation.49 | convolution fusion | flops 536870912 | bytes 29360128 | tf_op jit(solution)/shard_map/gjc,gcx->gjx/dot_general | solution.py:44
  95.9 21.2 %fusion.3 = f32[32,8192]{1,0:T(8,128)} fusion(f32[64,8,64,128]{3,2,1,0:T(8,128)} %bitcast.21, s32[512]{0:T(512)S(1)} %get-tuple-element.8, pred[512]{0:T(512)(128)(4,1)S(1)} %iota_compare_fusion.2), kind=kOutput, calls=%fused_computation.5 | convolution fusion | flops 1610645504 | bytes 17828352 | tf_op jit(solution)/shard_map/dot_general | solution.py:65
  117.1 0.0 all-reduce.3.cloned.1.call-update
  117.1 0.0 copy-start.1
  117.1 20.6 %fusion = f32[32,8192]{1,0:T(8,128)S(1)} fusion(f32[64,8,64,128]{3,2,1,0:T(8,128)} %bitcast.20, s32[512]{0:T(512)S(1)} %get-tuple-element.6, pred[512]{0:T(512)(128)(4,1)S(1)} %compare_and_fusion), kind=kOutput, calls=%fused_computation.2 | convolution fusion | flops 1610645504 | bytes 17828352 | tf_op jit(solution)/shard_map/dot_general | solution.py:59
  137.7 0.1 fusion.26
  137.8 1.9 %collective-permute-start.5 = (f32[8,8192]{1,0:T(8,128)S(1)}, f32[8,8192]{1,0:T(8,128)S(1)}, u32[]{:S(2)}, u32[]{:S(2)}) collective-permute-start(f32[8,8192]{1,0:T(8,128)S(1)} %get-tuple-element.9), channel_id=1, source_target_pairs={{0,4},{4,8},{8,12},{12,16},{16,20},{20,24},{24,28},{1,5},{5,9},{9,... | collective-permute-start | bytes 786440 | tf_op jit(solution)/shard_map/ppermute | solution.py:12
  139.7 4.3 %collective-permute-start.6 = (f32[8,8192]{1,0:T(8,128)S(1)}, f32[8,8192]{1,0:T(8,128)S(1)}, u32[]{:S(2)}, u32[]{:S(2)}) collective-permute-start(f32[8,8192]{1,0:T(8,128)S(1)} %get-tuple-element.11), channel_id=1, source_target_pairs={{0,8},{4,12},{8,16},{12,20},{16,24},{20,28},{1,9},{5,13},{9,17},{1... | collective-permute-start | bytes 786440 | tf_op jit(solution)/shard_map/ppermute | solution.py:12
  144.0 4.5 %collective-permute-start.7 = (f32[8,8192]{1,0:T(8,128)S(1)}, f32[8,8192]{1,0:T(8,128)S(1)}, u32[]{:S(2)}, u32[]{:S(2)}) collective-permute-start(f32[8,8192]{1,0:T(8,128)S(1)} %get-tuple-element.10), channel_id=1, source_target_pairs={{0,12},{4,16},{8,20},{12,24},{16,28},{1,13},{5,17},{9,21},{13,25},... | collective-permute-start | bytes 786440 | tf_op jit(solution)/shard_map/ppermute | solution.py:12
  148.5 0.6 dynamic-slice
  149.8 0.9 collective-permute-done.6
  150.6 5.6 %collective-permute-done.7 = f32[8,8192]{1,0:T(8,128)S(1)} collective-permute-done((f32[8,8192]{1,0:T(8,128)S(1)}, f32[8,8192]{1,0:T(8,128)S(1)}, u32[]{:S(2)}, u32[]{:S(2)}) %collective-permute-start.7) | collective-permute-done | bytes 262176 | tf_op jit(solution)/shard_map/ppermute | solution.py:12
  156.2 13.7 %all-reduce.3.cloned.1.call-done = f32[32,8192]{1,0:T(8,128)} async-done(((f32[32,8192]{1,0:T(8,128)}), f32[32,8192]{1,0:T(8,128)}) %all-reduce.3.cloned.1.call-update) | async-done | bytes 1048592
  169.9 1.0 fusion.9
  170.9 0.8 copy.11
  (15 shorter events, 0.1 us)
Async XLA Ops:
  6.5 25.3 %copy-start = (bf16[8,64,128]{2,1,0:T(8,128)(2,1)S(1)}, bf16[8,64,128]{2,1,0:T(8,128)(2,1)}, u32[]{:S(2)}) copy-start(bf16[8,64,128]{2,1,0:T(8,128)(2,1)} %param.5) | copy-start | bytes 393220
  6.5 163.4 %all-reduce.3.cloned.1.call-start = ((), (), s32[]{:S(2)}) async-start(), calls=%async_computation | async-start | bytes 2097152
  6.5 8.1 %collective-permute-start.2 = (bf16[8,64,128]{2,1,0:T(8,128)(2,1)}, bf16[8,64,128]{2,1,0:T(8,128)(2,1)S(1)}, u32[]{:S(2)}, u32[]{:S(2)}) collective-permute-start(bf16[8,64,128]{2,1,0:T(8,128)(2,1)} %param.5), channel_id=1, source_target_pairs={{0,1},{1,2},{2,3},{3,0},{4,5},{5,6},{6,7},{7,4},{8,9},{9,10},{10,1... | collective-permute-start | bytes 393224 | tf_op jit(solution)/shard_map/ppermute | solution.py:29
  9.5 22.3 %collective-permute-start = (bf16[8,64,128]{2,1,0:T(8,128)(2,1)}, bf16[8,64,128]{2,1,0:T(8,128)(2,1)S(1)}, u32[]{:S(2)}, u32[]{:S(2)}) collective-permute-start(bf16[8,64,128]{2,1,0:T(8,128)(2,1)} %param.5), channel_id=1, source_target_pairs={{4,0},{8,4},{12,8},{16,12},{20,16},{24,20},{28,24},{5,1},{9,5},{13... | collective-permute-start | bytes 393224 | tf_op jit(solution)/shard_map/ppermute | solution.py:12
  14.6 18.5 %collective-permute-start.3 = (bf16[8,64,128]{2,1,0:T(8,128)(2,1)S(1)}, bf16[8,64,128]{2,1,0:T(8,128)(2,1)S(1)}, u32[]{:S(2)}, u32[]{:S(2)}) collective-permute-start(bf16[8,64,128]{2,1,0:T(8,128)(2,1)S(1)} %collective-permute-done.2), channel_id=1, source_target_pairs={{0,1},{1,2},{2,3},{3,0},{4,5},{5,6},{6,7},{7,4},{8,9},{9,10},{10,1... | collective-permute-start | bytes 393224 | tf_op jit(solution)/shard_map/ppermute | solution.py:29
  31.9 36.0 %collective-permute-start.1 = (bf16[16,64,128]{2,1,0:T(8,128)(2,1)S(1)}, bf16[16,64,128]{2,1,0:T(8,128)(2,1)S(1)}, u32[]{:S(2)}, u32[]{:S(2)}) collective-permute-start(bf16[16,64,128]{2,1,0:T(8,128)(2,1)S(1)} %pad_maximum_fusion.1), channel_id=1, source_target_pairs={{8,0},{12,4},{16,8},{20,12},{24,16},{28,20},{9,1},{13,5},{17,9},{2... | collective-permute-start | bytes 786440 | tf_op jit(solution)/shard_map/ppermute | solution.py:12
  33.2 7.4 %collective-permute-start.4 = (bf16[8,64,128]{2,1,0:T(8,128)(2,1)S(1)}, bf16[8,64,128]{2,1,0:T(8,128)(2,1)S(1)}, u32[]{:S(2)}, u32[]{:S(2)}) collective-permute-start(bf16[8,64,128]{2,1,0:T(8,128)(2,1)S(1)} %collective-permute-done.3), channel_id=1, source_target_pairs={{0,1},{1,2},{2,3},{3,0},{4,5},{5,6},{6,7},{7,4},{8,9},{9,10},{10,1... | collective-permute-start | bytes 393224 | tf_op jit(solution)/shard_map/ppermute | solution.py:29
  117.1 31.4 %copy-start.1 = (u32[32]{0:T(128)S(1)}, u32[32]{0:T(128)}, u32[]{:S(2)}) copy-start(u32[32]{0:T(128)} %constant.79) | copy-start | bytes 388
  137.8 12.0 %collective-permute-start.5 = (f32[8,8192]{1,0:T(8,128)S(1)}, f32[8,8192]{1,0:T(8,128)S(1)}, u32[]{:S(2)}, u32[]{:S(2)}) collective-permute-start(f32[8,8192]{1,0:T(8,128)S(1)} %get-tuple-element.9), channel_id=1, source_target_pairs={{0,4},{4,8},{8,12},{12,16},{16,20},{20,24},{24,28},{1,5},{5,9},{9,... | collective-permute-start | bytes 786440 | tf_op jit(solution)/shard_map/ppermute | solution.py:12
  139.7 10.9 %collective-permute-start.6 = (f32[8,8192]{1,0:T(8,128)S(1)}, f32[8,8192]{1,0:T(8,128)S(1)}, u32[]{:S(2)}, u32[]{:S(2)}) collective-permute-start(f32[8,8192]{1,0:T(8,128)S(1)} %get-tuple-element.11), channel_id=1, source_target_pairs={{0,8},{4,12},{8,16},{12,20},{16,24},{20,28},{1,9},{5,13},{9,17},{1... | collective-permute-start | bytes 786440 | tf_op jit(solution)/shard_map/ppermute | solution.py:12
  144.0 12.2 %collective-permute-start.7 = (f32[8,8192]{1,0:T(8,128)S(1)}, f32[8,8192]{1,0:T(8,128)S(1)}, u32[]{:S(2)}, u32[]{:S(2)}) collective-permute-start(f32[8,8192]{1,0:T(8,128)S(1)} %get-tuple-element.10), channel_id=1, source_target_pairs={{0,12},{4,16},{8,20},{12,24},{16,28},{1,13},{5,17},{9,21},{13,25},... | collective-permute-start | bytes 786440 | tf_op jit(solution)/shard_map/ppermute | solution.py:12
Sparse Core Ops, SparseCore 0:
  117.2 52.6 all-reduce.2
